TPU v7x, 512 devices: a whole 4x8x8 slice. The times are simulated.
512 devices in a mesh: group: 64 (over y_lo, z, core), tensor: 8 (over y_hi, x).
Axes of the slice: x: 4, y: 8 (y_hi: 2, y_lo: 4; y = y_hi * 4 + y_lo), z: 8, core: 2. Of those that a mesh axis runs over, the one named last changes fastest.
Arguments:
- turns: bfloat16 [64, 1024, 4096], P('group', 'tensor'), may hold values from -16 to 16
- query_store: bfloat16 [64, 64, 4096], P('group', None, 'tensor'), may hold values from -0.09375 to 0.09375
- key_block_holder: bfloat16 [64, 64, 4, 128], P('group'), may hold values from -0.09375 to 0.09375
- value_block_holder: bfloat16 [64, 64, 4, 128], P('group'), may hold values from -0.09375 to 0.09375
- query_bias: float32 [4096], P('tensor'), may hold values from -3 to 3
- key_projection_bias: float32 [512], replicated, may hold values from -3 to 3
- value_projection_bias: float32 [512], replicated, may hold values from -3 to 3
- owner: int32 [64], replicated, may hold values from 0 to 63, each once
- lengths: int32 [64], P('group'), may hold values from 1 to 1024, as said below
Outputs:
- attended: bfloat16 [64, 1024, 4096], P('group', None, 'tensor')
Inputs may be any that keep to these rules, and one draw needn't show every extreme that they name: `owner`: each group index holds exactly one block. `lengths`: some group's turn fills all 1024 positions.
All inputs are finite; a program needn't handle non-finite values.
Results may differ from a plain program's by a relative error of at most 0.0055.
The roundings to bfloat16 on the way count: a program that leaves them out, or rounds other values in their place, can miss the bound.
Values may be sent and summed in bfloat16 or wider, within the bound.
No kernel may reach another device: no remote copies, remote signals or barrier semaphores. Data moves between devices by JAX's collectives and lax.ppermute only.
A program may use at most 128 MiB of HBM per device.

v0:
```python
import jax
import jax.numpy as jnp
from jax import lax
from jax.sharding import PartitionSpec as P

QUERY_HEADS = 32
KEY_VALUE_HEADS = 4
HEAD_SIZE = 128


rotary_base = 1000000.0


def rotary(heads, positions):
    half = heads.shape[-1] // 2
    expo = jnp.arange(half, dtype=jnp.float32) * 2.0 / heads.shape[-1]
    freqs = rotary_base ** (-expo)
    angles = positions[:, None] * freqs[None, :]
    cosine = jnp.cos(angles)[None]
    sine = jnp.sin(angles)[None]
    first = heads[..., :half]
    second = heads[..., half:]
    return jnp.concatenate(
        [first * cosine - second * sine, second * cosine + first * sine], axis=-1
    )


def per_device(
    turns,
    query_store,
    key_block_holder,
    value_block_holder,
    query_bias,
    key_projection_bias,
    value_projection_bias,
    owner,
    lengths,
):
    tensor_index = lax.axis_index("tensor")
    group_count = lax.axis_size("group")
    gathered = lax.all_gather(turns, "tensor", axis=1, tiled=True)[0]
    token_count = gathered.shape[0]
    block_rows = query_store.shape[1]
    query_cols = query_store.shape[2]
    heads_dev = query_cols // HEAD_SIZE
    query_per_key_head = QUERY_HEADS // KEY_VALUE_HEADS
    key_value_per_group = max(1, heads_dev // query_per_key_head)
    key_value_leading = tensor_index * heads_dev // query_per_key_head
    keys_mine = lax.dynamic_slice_in_dim(
        key_block_holder, key_value_leading, key_value_per_group, 2
    ).reshape(1, block_rows, key_value_per_group * HEAD_SIZE)
    values_mine = lax.dynamic_slice_in_dim(
        value_block_holder, key_value_leading, key_value_per_group, 2
    ).reshape(1, block_rows, key_value_per_group * HEAD_SIZE)
    inverse = (
        jnp.zeros((group_count,), jnp.int32).at[owner].set(jnp.arange(group_count, dtype=jnp.int32))
    )
    ordered = jnp.take(gathered.reshape(token_count, group_count, block_rows), inverse, axis=1)
    proj_query = jnp.einsum(
        "tgc,gcn->tn",
        ordered,
        lax.all_gather(query_store, "group", axis=0, tiled=True),
        preferred_element_type=jnp.float32,
    )
    proj_key = jnp.einsum(
        "tgc,gcn->tn",
        ordered,
        lax.all_gather(keys_mine, "group", axis=0, tiled=True),
        preferred_element_type=jnp.float32,
    )
    proj_value = jnp.einsum(
        "tgc,gcn->tn",
        ordered,
        lax.all_gather(values_mine, "group", axis=0, tiled=True),
        preferred_element_type=jnp.float32,
    )
    key_bias_rows = lax.dynamic_slice_in_dim(
        key_projection_bias.reshape(KEY_VALUE_HEADS, HEAD_SIZE),
        key_value_leading,
        key_value_per_group,
        0,
    ).reshape(key_value_per_group * HEAD_SIZE)
    bias_values = lax.dynamic_slice_in_dim(
        value_projection_bias.reshape(KEY_VALUE_HEADS, HEAD_SIZE),
        key_value_leading,
        key_value_per_group,
        0,
    ).reshape(key_value_per_group * HEAD_SIZE)
    positions = jnp.arange(token_count, dtype=jnp.float32)
    raw_query = (
        (proj_query + query_bias).reshape(token_count, heads_dev, HEAD_SIZE).transpose(1, 0, 2)
    )
    unbiased_key = (
        (proj_key + key_bias_rows)
        .reshape(token_count, key_value_per_group, HEAD_SIZE)
        .transpose(1, 0, 2)
    )
    unbiased_value = (
        (proj_value + bias_values)
        .reshape(token_count, key_value_per_group, HEAD_SIZE)
        .transpose(1, 0, 2)
    )
    queries = rotary(raw_query, positions).astype(jnp.bfloat16)
    keys_rot = rotary(unbiased_key, positions).astype(jnp.bfloat16)
    values_cast = unbiased_value.astype(jnp.bfloat16)
    repeat_count = heads_dev // key_value_per_group
    keys_full = jnp.repeat(keys_rot, repeat_count, axis=0)
    values_full = jnp.repeat(values_cast, repeat_count, axis=0)
    index = jnp.arange(token_count, dtype=jnp.int32)
    span = min(256, token_count)
    outputs = []
    for block in range(token_count // span):
        first = block * span
        last = first + span
        scores = jnp.einsum(
            "htd,hsd->hts",
            queries[:, first:last],
            keys_full[:, :last],
            preferred_element_type=jnp.float32,
        ) * HEAD_SIZE ** (-0.5)
        causal = index[None, :last] <= index[first:last, None]
        scores = jnp.where(causal[None], scores, -jnp.inf)
        top = jnp.max(scores, axis=-1, keepdims=True)
        expd = jnp.exp(scores - top)
        weights = (expd / jnp.sum(expd, axis=-1, keepdims=True)).astype(jnp.bfloat16)
        outputs.append(
            jnp.einsum(
                "hts,hsd->htd", weights, values_full[:, :last], preferred_element_type=jnp.float32
            )
        )
    mixed = jnp.concatenate(outputs, axis=1)
    mixed = mixed.transpose(1, 0, 2).reshape(token_count, query_cols)
    live = (index < lengths[0])[:, None]
    return jnp.where(live, mixed, 0.0).astype(jnp.bfloat16)[None]


def solution(mesh):
    in_specs = (
        P("group", "tensor", None),
        P("group", None, "tensor"),
        P("group", None, None, None),
        P("group", None, None, None),
        P("tensor"),
        P(),
        P(),
        P(),
        P("group"),
    )
    out_specs = P("group", None, "tensor")
    return jax.shard_map(
        per_device, mesh=mesh, in_specs=in_specs, out_specs=out_specs, check_vma=False
    )
```

profile of v0, /device:TPU:57, one launch (start us, length us, event | category | flops | bytes accessed | tf_op | source)
XLA Modules:
  0.0 599.4 jit_solution(14467278969102455105)
XLA Ops:
  6.5 2.3 copy.34
  11.1 0.8 scatter_custom_fusion
  12.0 2.9 fusion.55
  15.0 0.9 iota_compare_fusion
  17.3 0.8 broadcast_compare_fusion.1
  18.1 0.8 broadcast_compare_fusion
  18.9 167.7 %all-gather.7.cloned.1.call-done = bf16[1,1024,4096]{1,2,0:T(8,128)(2,1)} async-done(((bf16[1,128,4096]{1,2,0:T(8,128)(2,1)}), bf16[1,1024,4096]{1,2,0:T(8,128)(2,1)}) %all-gather.7.cloned.1.call-update) | async-done | bytes 8388624 | tf_op jit(solution)/shard_map/all_gather | solution.py:41
  186.7 8.9 %gather_fusion = bf16[64,1024,64]{1,2,0:T(8,128)(2,1)} fusion(bf16[1024,64,64]{0,2,1:T(8,128)(2,1)} %bitcast.67, s32[1024]{0:T(1024)S(1)} %pad_clamp_fusion), kind=kCustom, calls=%fused_computation | custom fusion | bytes 16777472 | tf_op jit(solution)/shard_map/jit(_take)/gather | solution.py:58
  195.6 122.6 %all-gather.11.cloned.1.call-done = bf16[64,64,1,128]{3,1,2,0:T(8,128)(2,1)} async-done(((bf16[1,64,1,128]{3,1,2,0:T(8,128)(2,1)}), bf16[64,64,1,128]{3,1,2,0:T(8,128)(2,1)}) %all-gather.11.cloned.1.call-update) | async-done | bytes 1048592 | tf_op jit(solution)/shard_map/all_gather | solution.py:68
  318.2 5.0 fusion.36
  323.3 1.2 fusion.84
  325.2 112.7 %all-gather.9.cloned.1.call-done = bf16[64,64,512]{2,1,0:T(8,128)(2,1)} async-done(((bf16[1,64,512]{2,1,0:T(8,128)(2,1)}), bf16[64,64,512]{2,1,0:T(8,128)(2,1)}) %all-gather.9.cloned.1.call-update) | async-done | bytes 4194320 | tf_op jit(solution)/shard_map/all_gather | solution.py:62
  437.9 10.5 %bitcast_add_fusion = f32[1024,512]{0,1:T(8,128)} fusion(bf16[64,64,512]{2,1,0:T(8,128)(2,1)} %all-gather.9.cloned.1.call-done, f32[512]{0:T(512)S(1)} %copy-done.9, bf16[64,1024,64]{1,2,0:T(8,128)(2,1)} %gather_fusion, pred[64]{0:T(512)(128)(4,1)S(1)} %compare_and_fusion), kind=kOutput, calls=%fused_computation.24 | convolution fusion | flops 4299685888 | bytes 14682176 | tf_op jit(solution)/shard_map/tgc,gcn->tn/dot_general | solution.py:59
  448.3 2.1 copy.35
  451.1 2.9 subtract_convert_fusion
  454.0 1.6 fusion.138
  455.6 1.2 fusion.26
  456.9 98.5 %all-gather.13.cloned.1.call-done = bf16[64,64,1,128]{3,1,2,0:T(8,128)(2,1)} async-done(((bf16[1,64,1,128]{3,1,2,0:T(8,128)(2,1)}), bf16[64,64,1,128]{3,1,2,0:T(8,128)(2,1)}) %all-gather.13.cloned.1.call-update) | async-done | bytes 1048592 | tf_op jit(solution)/shard_map/all_gather | solution.py:74
  555.3 6.4 %fusion.42 = bf16[1024,128]{1,0:T(8,128)(2,1)S(1)} fusion(bf16[64,64,1,128]{3,1,2,0:T(8,128)(2,1)} %all-gather.13.cloned.1.call-done, f32[128]{0:T(128)S(1)} %get-tuple-element.16, bf16[64,1024,64]{1,2,0:T(8,128)(2,1)} %gather_fusion, pred[64]{0:T(512)(128)(4,1)S(1)} %compare_and_fusion), kind=kOutput, calls=%fused_computation.48 | convolution fusion | flops 1078198272 | bytes 9699904 | tf_op jit(solution)/shard_map/tgc,gcn->tn/dot_general | solution.py:71
  561.8 0.7 fusion.80
  563.3 1.7 copy.40
  564.9 1.1 copy.41
  566.0 2.3 fusion.58
  568.3 1.1 copy.42
  569.5 2.7 fusion.52
  572.2 2.0 fusion.133
  574.2 3.6 fusion.50
  577.8 6.1 %fusion.132 = (f32[4,256]{1,0:T(4,128)S(1)}, f32[4,256,768]{2,1,0:T(8,128)}) fusion(f32[4,256,768]{2,1,0:T(8,128)} %fusion.58, pred[256,768]{1,0:T(8,128)(4,1)} %broadcast_compare_fusion), kind=kOutput, calls=%fused_computation.136 | output fusion | flops 4719359 | bytes 6492160 | tf_op jit(solution)/shard_map/sub | solution.py:124
  584.0 2.0 fusion.131
  586.0 1.1 fusion.16
  588.1 2.6 fusion.23
  591.6 1.3 copy.44
  (66 shorter events, 7.0 us)
Async XLA Ops:
  6.5 2.4 copy-start
  6.5 3.9 copy-start.8
  6.5 4.6 copy-start.10
  6.5 180.1 %all-gather.7.cloned.1.call-start = ((), (), s32[]{:S(2)}) async-start(), calls=%async_computation | async-start | bytes 9437184 | tf_op jit(solution)/shard_map/all_gather | solution.py:41
  8.9 309.4 %all-gather.11.cloned.1.call-start = ((), (), s32[]{:S(2)}) async-start(), calls=%async_computation.2 | async-start | bytes 1064960 | tf_op jit(solution)/shard_map/all_gather | solution.py:68
  9.6 428.3 %all-gather.9.cloned.1.call-start = ((), (), s32[]{:S(2)}) async-start(), calls=%async_computation.1 | async-start | bytes 4259840 | tf_op jit(solution)/shard_map/all_gather | solution.py:62
  10.4 545.0 %all-gather.13.cloned.1.call-start = ((), (), s32[]{:S(2)}) async-start(), calls=%async_computation.3 | async-start | bytes 1064960 | tf_op jit(solution)/shard_map/all_gather | solution.py:74
  318.2 119.7 %copy-start.9 = (f32[512]{0:T(512)S(1)}, f32[512]{0:T(512)}, u32[]{:S(2)}) copy-start(f32[512]{0:T(512)} %param.13) | copy-start | bytes 6148
  454.0 1.6 copy-start.1
  561.8 0.8 copy-start.3
  572.2 2.0 slice-start.1
  572.2 2.0 copy-start.7
  577.8 6.1 %copy-start.2 = (f32[4,256,1024]{2,1,0:T(8,128)S(1)}, f32[4,256,1024]{2,1,0:T(8,128)}, u32[]{:S(2)}) copy-start(f32[4,256,1024]{2,1,0:T(8,128)} %fusion.52) | copy-start | bytes 12582916
  577.8 6.1 %copy-start.5 = (pred[256,1024]{1,0:T(8,128)(4,1)S(1)}, pred[256,1024]{1,0:T(8,128)(4,1)}, u32[]{:S(2)}) copy-start(pred[256,1024]{1,0:T(8,128)(4,1)} %iota_compare_fusion) | copy-start | bytes 786436
  584.0 2.1 copy-start.4
  586.0 1.1 slice-start
  587.1 0.9 slice-start.2
  588.1 2.6 copy-start.6
Sparse Core Ops, SparseCore 0:
  10.4 176.2 all-gather.6
  188.8 129.3 all-gather.10
  320.4 117.4 all-gather.8
  439.9 115.4 all-gather.12
where the time goes:
time: 600 us; the launch traced here: 599 us
  waiting for transfers between devices  502 us (84%)
  matrix products  39.6 us (7%)
  local copies, waits for them, and re-layouts  23.1 us (4%)
  other arithmetic  20.3 us (3%)
  between operations  14.1 us (2%)
    all_gather x1, waiting for transfers between devices, per_device(): gathered = lax.all_gather(turns, 'tensor', axis=1, tiled=True)[0]  168 us
    all_gather x1, waiting for transfers between devices, per_device(): lax.all_gather(keys_mine, 'group', axis=0, tiled=True)  123 us
    all_gather x1, waiting for transfers between devices, per_device(): lax.all_gather(query_store, 'group', axis=0, tiled=True)  113 us
    all_gather x1, waiting for transfers between devices, per_device(): lax.all_gather(values_mine, 'group', axis=0, tiled=True)  98.5 us
  transfers between devices with their start and end apart: 4, of which 4 were waited for; matrix products, arithmetic and copies ran while one was open for 7% of the time, Pallas kernels for 0%

commit v1 on v0

v1 whole, which is shorter than its diff:
```python
import functools

import jax
import jax.numpy as jnp
from jax import lax
from jax.experimental import pallas as pl
from jax.experimental.pallas import tpu as pltpu
from jax.sharding import PartitionSpec as P


HEAD_SIZE = 128
FEATURES = 4096
TOKENS = 1024
GROUPS = 64
ROWS = 64
HEADS_DEV = 4
QCOLS = HEADS_DEV * HEAD_SIZE
COLS = QCOLS + 2 * HEAD_SIZE
SPAN = 256
rotary_base = 1000000.0


def group_perm(dy=0, dz=0, dc=0):
    out = []
    for g in range(64):
        y, z, c = g // 16, (g // 2) % 8, g % 2
        out.append((g, ((y + dy) % 4) * 16 + ((z + dz) % 8) * 2 + (c + dc) % 2))
    return out


def tensor_perm(dy=0, dx=0):
    return [(t, ((t // 4 + dy) % 2) * 4 + (t % 4 + dx) % 4) for t in range(8)]


def send_group(a, **k):
    return lax.ppermute(a, "group", group_perm(**k))


def send_tensor(a, **k):
    return lax.ppermute(a, "tensor", tensor_perm(**k))


def kernel(
    n_pieces,
    row_ref,
    pos_ref,
    len_ref,
    *refs,
):
    pieces = refs[:n_pieces]
    w_mine, w_other, bias_ref, cos_ref, sin_ref, out_ref = refs[n_pieces : n_pieces + 6]
    x_buf, w_buf, q_buf, k_buf, v_buf, x_sem, w_sem = refs[n_pieces + 6 :]

    def fetch(b, carry):
        p = pos_ref[b]
        dst = w_buf.at[pl.ds(pl.multiple_of(b * ROWS, ROWS), ROWS), :]

        @pl.when(p < 32)
        def _():
            pltpu.make_async_copy(w_mine.at[p], dst, w_sem).start()

        @pl.when(p >= 32)
        def _():
            pltpu.make_async_copy(w_other.at[p - 32], dst, w_sem).start()

        return carry

    lax.fori_loop(0, GROUPS, fetch, 0)
    for i, piece in enumerate(pieces):
        first = pl.multiple_of(row_ref[i], 32)
        pltpu.make_async_copy(piece, x_buf.at[pl.ds(first, piece.shape[0]), :], x_sem).start()
    pltpu.make_async_copy(w_buf, w_buf, w_sem).wait()
    pltpu.make_async_copy(x_buf, x_buf, x_sem).wait()

    def project(i, carry):
        rows = pl.ds(pl.multiple_of(i * SPAN, SPAN), SPAN)
        acc = jnp.dot(x_buf[rows, :], w_buf[...], preferred_element_type=jnp.float32)
        acc = acc + bias_ref[...]
        cos, sin = cos_ref[rows, :], sin_ref[rows, :]
        for h in range(HEADS_DEV + 1):
            a = acc[:, h * HEAD_SIZE : (h + 1) * HEAD_SIZE]
            r = (a * cos + pltpu.roll(a, HEAD_SIZE // 2, 1) * sin).astype(jnp.bfloat16)
            if h < HEADS_DEV:
                q_buf[h, rows, :] = r
            else:
                k_buf[rows, :] = r
        v_buf[rows, :] = acc[:, (HEADS_DEV + 1) * HEAD_SIZE :].astype(jnp.bfloat16)
        return carry

    lax.fori_loop(0, TOKENS // SPAN, project, 0)

    scale = HEAD_SIZE ** (-0.5)
    live_len = len_ref[0]
    for i in range(TOKENS // SPAN):
        first, last = i * SPAN, (i + 1) * SPAN
        keys = k_buf[:last, :]
        values = v_buf[:last, :]
        qpos = first + lax.broadcasted_iota(jnp.int32, (SPAN, last), 0)
        kpos = lax.broadcasted_iota(jnp.int32, (SPAN, last), 1)
        causal = kpos <= qpos
        live = first + lax.broadcasted_iota(jnp.int32, (SPAN, HEAD_SIZE), 0) < live_len

        def attend(h, carry):
            q = q_buf[h, first:last, :]
            s = lax.dot_general(
                q, keys, (((1,), (1,)), ((), ())), preferred_element_type=jnp.float32
            )
            s = jnp.where(causal, s * scale, -jnp.inf)
            top = jnp.max(s, axis=-1, keepdims=True)
            e = jnp.exp(s - top)
            w = (e * (1.0 / jnp.sum(e, axis=-1, keepdims=True))).astype(jnp.bfloat16)
            o = jnp.dot(w, values, preferred_element_type=jnp.float32)
            o = jnp.where(live, o, 0.0).astype(jnp.bfloat16)
            out_ref[first:last, pl.ds(pl.multiple_of(h * HEAD_SIZE, HEAD_SIZE), HEAD_SIZE)] = o
            return carry

        lax.fori_loop(0, HEADS_DEV, attend, 0)


def per_device(
    turns,
    query_store,
    key_block_holder,
    value_block_holder,
    query_bias,
    key_projection_bias,
    value_projection_bias,
    owner,
    lengths,
):
    t = lax.axis_index("tensor")
    g = lax.axis_index("group")
    my_y, my_z, my_c = g // 16, (g // 2) % 8, g % 2
    my_x, my_h = t % 4, t // 4
    head = t // 2

    kv = [
        lax.dynamic_slice_in_dim(b, head, 1, 2).reshape(1, ROWS, HEAD_SIZE)
        for b in (key_block_holder, value_block_holder)
    ]
    block = jnp.concatenate([query_store] + kv, axis=2)
    bias = jnp.concatenate(
        [query_bias]
        + [
            lax.dynamic_slice_in_dim(b, head * HEAD_SIZE, HEAD_SIZE, 0)
            for b in (key_projection_bias, value_projection_bias)
        ]
    ).reshape(1, COLS)

    quad = jnp.concatenate([block] + [send_group(block, dy=d) for d in (1, 2, 3)], axis=0)
    ring = {0: quad}
    up = down = quad
    for e in (1, 2, 3):
        up = send_group(up, dz=1)
        down = send_group(down, dz=-1)
        ring[e], ring[8 - e] = up, down
    ring[4] = send_group(up, dz=1)
    w_mine = jnp.concatenate([ring[e] for e in range(8)], axis=0)
    w_other = send_group(w_mine, dc=1)

    mine = turns[0]
    half = mine.shape[0] // 2
    left = send_tensor(mine, dx=1)
    right = send_tensor(mine, dx=-1)
    parts = [
        (mine, 0, 0, 0),
        (left, 0, -1, 0),
        (right, 0, 1, 0),
        (send_tensor(left[:half], dx=1), 0, 2, 0),
        (send_tensor(right[half:], dx=-1), 0, 2, half),
    ]
    for k in (0, 1):
        part = send_tensor(mine[k * half : (k + 1) * half], dy=1)
        left = send_tensor(part, dx=1)
        right = send_tensor(part, dx=-1)
        last = send_tensor((left, right)[k], dx=(1, -1)[k])
        parts += [(a, 1, dx, k * half) for a, dx in ((part, 0), (left, -1), (right, 1), (last, 2))]
    pieces = [p[0] for p in parts]
    firsts = [(((my_h + dh) % 2) * 4 + (my_x + dx) % 4) * 128 + row for _, dh, dx, row in parts]
    firsts = jnp.stack(firsts).astype(jnp.int32)

    o = owner.astype(jnp.int32)
    pos = (
        ((my_z - (o // 2) % 8) % 8) * 4 + (my_y - o // 16) % 4 + jnp.where(o % 2 == my_c, 0, 32)
    ).astype(jnp.int32)

    half_size = HEAD_SIZE // 2
    expo = jnp.arange(half_size, dtype=jnp.float32) * 2.0 / HEAD_SIZE
    freqs = rotary_base ** (-expo)
    angles = jnp.arange(TOKENS, dtype=jnp.float32)[:, None] * freqs[None, :]
    cosine, sine = jnp.cos(angles), jnp.sin(angles)
    cos = jnp.concatenate([cosine, cosine], axis=1)
    sin = jnp.concatenate([-sine, sine], axis=1)

    hbm = pl.BlockSpec(memory_space=pl.ANY)
    vmem = pl.BlockSpec(memory_space=pltpu.VMEM)
    out = pl.pallas_call(
        functools.partial(kernel, len(pieces)),
        out_shape=jax.ShapeDtypeStruct((TOKENS, QCOLS), jnp.bfloat16),
        grid_spec=pltpu.PrefetchScalarGridSpec(
            num_scalar_prefetch=3,
            grid=(),
            in_specs=[hbm] * (len(pieces) + 2) + [vmem] * 3,
            out_specs=vmem,
            scratch_shapes=[
                pltpu.VMEM((TOKENS, FEATURES), jnp.bfloat16),
                pltpu.VMEM((FEATURES, COLS), jnp.bfloat16),
                pltpu.VMEM((HEADS_DEV, TOKENS, HEAD_SIZE), jnp.bfloat16),
                pltpu.VMEM((TOKENS, HEAD_SIZE), jnp.bfloat16),
                pltpu.VMEM((TOKENS, HEAD_SIZE), jnp.bfloat16),
                pltpu.SemaphoreType.DMA(()),
                pltpu.SemaphoreType.DMA(()),
            ],
        ),
        compiler_params=pltpu.CompilerParams(vmem_limit_bytes=40 << 20),
        name="project_attend",
    )(firsts, pos, lengths.astype(jnp.int32), *pieces, w_mine, w_other, bias, cos, sin)
    return out[None]


def solution(mesh):
    in_specs = (
        P("group", "tensor", None),
        P("group", None, "tensor"),
        P("group", None, None, None),
        P("group", None, None, None),
        P("tensor"),
        P(),
        P(),
        P(),
        P("group"),
    )
    out_specs = P("group", None, "tensor")

    def step(*args):
        return per_device(*args)

    step = jax.shard_map(
        step, mesh=mesh, in_specs=in_specs, out_specs=out_specs, check_vma=False
    )
    return step
```

time: 600 us -> 217 us (0.36)
  the two profiles are of different devices: /device:TPU:57 before, /device:TPU:1 now
where the time goes in v1:
time: 217 us; the launch traced here: 216 us
  waiting for transfers between devices  95.7 us (44%)
  starting transfers between devices  79.9 us (37%)
  Pallas kernels  23.9 us (11%)
  local copies, waits for them, and re-layouts  10.2 us (5%)
  other arithmetic  4.71 us (2%)
    ppermute x12, waiting for transfers between devices, send_tensor(): return lax.ppermute(a, 'tensor', tensor_perm(**k))  66.4 us
    ppermute x11, starting transfers between devices, send_group(): return lax.ppermute(a, 'group', group_perm(**k))  40.2 us
    ppermute x12, starting transfers between devices, send_tensor(): return lax.ppermute(a, 'tensor', tensor_perm(**k))  39.7 us
    ppermute x11, waiting for transfers between devices, send_group(): return lax.ppermute(a, 'group', group_perm(**k))  29.3 us
    pallas_call x1, Pallas kernels, per_device(): pl.pallas_call(functools.partial(kernel, len(pieces)), out_shape=jax.Shap...  23.9 us
    unnamed x17, local copies, waits for them, and re-layouts  6.67 us
  transfers between devices with their start and end apart: 23, of which 12 were waited for; matrix products, arithmetic and copies ran while one was open for 4% of the time, Pallas kernels for 0%

profile of v1, /device:TPU:1, one launch (start us, length us, event | category | flops | bytes accessed | tf_op | source)
XLA Modules:
  0.0 215.7 jit_solution(9186791359052960829)
XLA Ops:
  2.5 4.0 %collective-permute-start.12 = (bf16[1,64,768]{2,1,0:T(8,128)(2,1)S(1)}, bf16[1,64,768]{2,1,0:T(8,128)(2,1)S(1)}, u32[]{:S(2)}, u32[]{:S(2)}) collective-permute-start(bf16[1,64,768]{2,1,0:T(8,128)(2,1)S(1)} %get-tuple-element.7), channel_id=1, source_target_pairs={{0,128},{8,136},{16,144},{24,152},{32,160},{40,168},{48,176},{56,1... | collective-permute-start | bytes 294920 | tf_op jit(solution)/shard_map/ppermute | solution.py:36
  6.5 4.2 %collective-permute-start.13 = (bf16[1,64,768]{2,1,0:T(8,128)(2,1)S(1)}, bf16[1,64,768]{2,1,0:T(8,128)(2,1)S(1)}, u32[]{:S(2)}, u32[]{:S(2)}) collective-permute-start(bf16[1,64,768]{2,1,0:T(8,128)(2,1)S(1)} %get-tuple-element.7), channel_id=1, source_target_pairs={{0,256},{8,264},{16,272},{24,280},{32,288},{40,296},{48,304},{56,3... | collective-permute-start | bytes 294920 | tf_op jit(solution)/shard_map/ppermute | solution.py:36
  10.7 3.0 %collective-permute-start.14 = (bf16[1,64,768]{2,1,0:T(8,128)(2,1)S(1)}, bf16[1,64,768]{2,1,0:T(8,128)(2,1)S(1)}, u32[]{:S(2)}, u32[]{:S(2)}) collective-permute-start(bf16[1,64,768]{2,1,0:T(8,128)(2,1)S(1)} %get-tuple-element.7), channel_id=1, source_target_pairs={{0,384},{8,392},{16,400},{24,408},{32,416},{40,424},{48,432},{56,4... | collective-permute-start | bytes 294920 | tf_op jit(solution)/shard_map/ppermute | solution.py:36
  13.7 4.6 %collective-permute-done.14 = bf16[1,64,768]{2,1,0:T(8,128)(2,1)S(1)} collective-permute-done((bf16[1,64,768]{2,1,0:T(8,128)(2,1)S(1)}, bf16[1,64,768]{2,1,0:T(8,128)(2,1)S(1)}, u32[]{:S(2)}, u32[]{:S(2)}) %collective-permute-start.14) | collective-permute-done | bytes 98336 | tf_op jit(solution)/shard_map/ppermute | solution.py:36
  19.2 2.9 %collective-permute-start.15 = (bf16[4,64,768]{2,1,0:T(8,128)(2,1)S(1)}, bf16[4,64,768]{2,1,0:T(8,128)(2,1)S(1)}, u32[]{:S(2)}, u32[]{:S(2)}) collective-permute-start(bf16[4,64,768]{2,1,0:T(8,128)(2,1)S(1)} %pad_maximum_fusion.2), channel_id=1, source_target_pairs={{0,16},{8,24},{16,32},{24,40},{32,48},{40,56},{48,64},{56,72},{64,... | collective-permute-start | bytes 1179656 | tf_op jit(solution)/shard_map/ppermute | solution.py:36
  22.1 14.7 %collective-permute-done.15 = bf16[4,64,768]{2,1,0:T(8,128)(2,1)S(1)} collective-permute-done((bf16[4,64,768]{2,1,0:T(8,128)(2,1)S(1)}, bf16[4,64,768]{2,1,0:T(8,128)(2,1)S(1)}, u32[]{:S(2)}, u32[]{:S(2)}) %collective-permute-start.15) | collective-permute-done | bytes 393248 | tf_op jit(solution)/shard_map/ppermute | solution.py:36
  38.7 4.6 %collective-permute-start.19 = (bf16[4,64,768]{2,1,0:T(8,128)(2,1)S(1)}, bf16[4,64,768]{2,1,0:T(8,128)(2,1)S(1)}, u32[]{:S(2)}, u32[]{:S(2)}) collective-permute-start(bf16[4,64,768]{2,1,0:T(8,128)(2,1)S(1)} %pad_maximum_fusion.2), channel_id=1, source_target_pairs={{0,112},{8,120},{16,0},{24,8},{32,16},{40,24},{48,32},{56,40},{64,... | collective-permute-start | bytes 1179656 | tf_op jit(solution)/shard_map/ppermute | solution.py:36
  43.3 5.3 %collective-permute-done.16 = bf16[4,64,768]{2,1,0:T(8,128)(2,1)S(1)} collective-permute-done((bf16[4,64,768]{2,1,0:T(8,128)(2,1)S(1)}, bf16[4,64,768]{2,1,0:T(8,128)(2,1)S(1)}, u32[]{:S(2)}, u32[]{:S(2)}) %collective-permute-start.16) | collective-permute-done | bytes 393248 | tf_op jit(solution)/shard_map/ppermute | solution.py:36
  48.6 1.9 collective-permute-start.17
  50.5 4.6 %collective-permute-start.20 = (bf16[4,64,768]{2,1,0:T(8,128)(2,1)S(1)}, bf16[4,64,768]{2,1,0:T(8,128)(2,1)S(1)}, u32[]{:S(2)}, u32[]{:S(2)}) collective-permute-start(bf16[4,64,768]{2,1,0:T(8,128)(2,1)S(1)} %collective-permute-done.19), channel_id=1, source_target_pairs={{0,112},{8,120},{16,0},{24,8},{32,16},{40,24},{48,32},{56,40},{64,... | collective-permute-start | bytes 1179656 | tf_op jit(solution)/shard_map/ppermute | solution.py:36
  56.4 3.1 %collective-permute-done.17 = bf16[4,64,768]{2,1,0:T(8,128)(2,1)S(1)} collective-permute-done((bf16[4,64,768]{2,1,0:T(8,128)(2,1)S(1)}, bf16[4,64,768]{2,1,0:T(8,128)(2,1)S(1)}, u32[]{:S(2)}, u32[]{:S(2)}) %collective-permute-start.17) | collective-permute-done | bytes 393248 | tf_op jit(solution)/shard_map/ppermute | solution.py:36
  62.1 4.6 %collective-permute-start.21 = (bf16[4,64,768]{2,1,0:T(8,128)(2,1)S(1)}, bf16[4,64,768]{2,1,0:T(8,128)(2,1)S(1)}, u32[]{:S(2)}, u32[]{:S(2)}) collective-permute-start(bf16[4,64,768]{2,1,0:T(8,128)(2,1)S(1)} %collective-permute-done.20), channel_id=1, source_target_pairs={{0,112},{8,120},{16,0},{24,8},{32,16},{40,24},{48,32},{56,40},{64,... | collective-permute-start | bytes 1179656 | tf_op jit(solution)/shard_map/ppermute | solution.py:36
  73.7 6.7 %collective-permute-start.22 = (bf16[32,64,768]{2,1,0:T(8,128)(2,1)}, bf16[32,64,768]{2,1,0:T(8,128)(2,1)}, u32[]{:S(2)}, u32[]{:S(2)}) collective-permute-start(bf16[32,64,768]{2,1,0:T(8,128)(2,1)} %constant_dynamic-update-slice_fusion.refs_13_), channel_id=1, source_target_pairs={{0,8},{8,0},{16,24},{24,16},{32,40},{40,32},{48,56},{56,48},{64,72... | collective-permute-start | bytes 9437192 | tf_op jit(solution)/shard_map/ppermute | solution.py:36
  80.4 3.1 %collective-permute-start = (bf16[128,4096]{1,0:T(8,128)(2,1)S(1)}, bf16[128,4096]{1,0:T(8,128)(2,1)S(1)}, u32[]{:S(2)}, u32[]{:S(2)}) collective-permute-start(bf16[128,4096]{1,0:T(8,128)(2,1)S(1)} %bitcast.25), channel_id=1, source_target_pairs={{0,1},{1,2},{2,3},{3,0},{4,5},{5,6},{6,7},{7,4},{8,9},{9,10},{10,1... | collective-permute-start | bytes 3145736 | tf_op jit(solution)/shard_map/ppermute | solution.py:40
  83.6 3.4 %collective-permute-start.1 = (bf16[128,4096]{1,0:T(8,128)(2,1)S(1)}, bf16[128,4096]{1,0:T(8,128)(2,1)S(1)}, u32[]{:S(2)}, u32[]{:S(2)}) collective-permute-start(bf16[128,4096]{1,0:T(8,128)(2,1)S(1)} %bitcast.26), channel_id=1, source_target_pairs={{0,3},{1,0},{2,1},{3,2},{4,7},{5,4},{6,5},{7,6},{8,11},{9,8},{10,9... | collective-permute-start | bytes 3145736 | tf_op jit(solution)/shard_map/ppermute | solution.py:40
  87.0 9.7 %collective-permute-start.8 = (bf16[64,4096]{1,0:T(8,128)(2,1)S(1)}, bf16[64,4096]{1,0:T(8,128)(2,1)}, u32[]{:S(2)}, u32[]{:S(2)}) collective-permute-start(bf16[64,4096]{1,0:T(8,128)(2,1)S(1)} %get-tuple-element.5), channel_id=1, source_target_pairs={{0,4},{1,5},{2,6},{3,7},{4,0},{5,1},{6,2},{7,3},{8,12},{9,13},{10,... | collective-permute-start | bytes 1572872 | tf_op jit(solution)/shard_map/ppermute | solution.py:40
  96.7 1.9 collective-permute-start.4
  98.7 26.9 %collective-permute-done.8.refs_9_ = bf16[64,4096]{1,0:T(8,128)(2,1)} collective-permute-done((bf16[64,4096]{1,0:T(8,128)(2,1)S(1)}, bf16[64,4096]{1,0:T(8,128)(2,1)}, u32[]{:S(2)}, u32[]{:S(2)}) %collective-permute-start.8) | collective-permute-done | bytes 524320 | tf_op jit(solution)/shard_map/ppermute | solution.py:40
  125.6 3.2 %collective-permute-start.10 = (bf16[64,4096]{1,0:T(8,128)(2,1)}, bf16[64,4096]{1,0:T(8,128)(2,1)}, u32[]{:S(2)}, u32[]{:S(2)}) collective-permute-start(bf16[64,4096]{1,0:T(8,128)(2,1)} %collective-permute-done.8.refs_9_), channel_id=1, source_target_pairs={{0,3},{1,0},{2,1},{3,2},{4,7},{5,4},{6,5},{7,6},{8,11},{9,8},{10,9... | collective-permute-start | bytes 1572872 | tf_op jit(solution)/shard_map/ppermute | solution.py:40
  128.8 13.7 %collective-permute-done.4.refs_5_ = bf16[64,4096]{1,0:T(8,128)(2,1)} collective-permute-done((bf16[64,4096]{1,0:T(8,128)(2,1)S(1)}, bf16[64,4096]{1,0:T(8,128)(2,1)}, u32[]{:S(2)}, u32[]{:S(2)}) %collective-permute-start.4) | collective-permute-done | bytes 524320 | tf_op jit(solution)/shard_map/ppermute | solution.py:40
  142.4 1.9 collective-permute-start.5
  144.4 4.6 %collective-permute-start.6 = (bf16[64,4096]{1,0:T(8,128)(2,1)}, bf16[64,4096]{1,0:T(8,128)(2,1)}, u32[]{:S(2)}, u32[]{:S(2)}) collective-permute-start(bf16[64,4096]{1,0:T(8,128)(2,1)} %collective-permute-done.4.refs_5_), channel_id=1, source_target_pairs={{0,3},{1,0},{2,1},{3,2},{4,7},{5,4},{6,5},{7,6},{8,11},{9,8},{10,9... | collective-permute-start | bytes 1572872 | tf_op jit(solution)/shard_map/ppermute | solution.py:40
  149.0 1.9 collective-permute-start.9
  153.5 1.9 collective-permute-start.2
  155.4 2.7 %collective-permute-done.5.refs_6_ = bf16[64,4096]{1,0:T(8,128)(2,1)} collective-permute-done((bf16[64,4096]{1,0:T(8,128)(2,1)}, bf16[64,4096]{1,0:T(8,128)(2,1)}, u32[]{:S(2)}, u32[]{:S(2)}) %collective-permute-start.5) | collective-permute-done | bytes 524320 | tf_op jit(solution)/shard_map/ppermute | solution.py:40
  158.1 2.0 collective-permute-start.3
  160.1 4.2 %collective-permute-start.11 = (bf16[64,4096]{1,0:T(8,128)(2,1)}, bf16[64,4096]{1,0:T(8,128)(2,1)S(1)}, u32[]{:S(2)}, u32[]{:S(2)}) collective-permute-start(bf16[64,4096]{1,0:T(8,128)(2,1)} %collective-permute-done.10.refs_11_), channel_id=1, source_target_pairs={{0,3},{1,0},{2,1},{3,2},{4,7},{5,4},{6,5},{7,6},{8,11},{9,8},{10,9... | collective-permute-start | bytes 1572872 | tf_op jit(solution)/shard_map/ppermute | solution.py:40
  164.4 5.0 %collective-permute-done.9.refs_10_ = bf16[64,4096]{1,0:T(8,128)(2,1)} collective-permute-done((bf16[64,4096]{1,0:T(8,128)(2,1)}, bf16[64,4096]{1,0:T(8,128)(2,1)}, u32[]{:S(2)}, u32[]{:S(2)}) %collective-permute-start.9) | collective-permute-done | bytes 524320 | tf_op jit(solution)/shard_map/ppermute | solution.py:40
  171.3 2.0 fusion.2
  173.6 7.4 %collective-permute-done.11.refs_12_ = bf16[64,4096]{1,0:T(8,128)(2,1)S(1)} collective-permute-done((bf16[64,4096]{1,0:T(8,128)(2,1)}, bf16[64,4096]{1,0:T(8,128)(2,1)S(1)}, u32[]{:S(2)}, u32[]{:S(2)}) %collective-permute-start.11) | collective-permute-done | bytes 524320 | tf_op jit(solution)/shard_map/ppermute | solution.py:40
  181.0 10.7 %collective-permute-done.7.refs_8_ = bf16[64,4096]{1,0:T(8,128)(2,1)S(1)} collective-permute-done((bf16[64,4096]{1,0:T(8,128)(2,1)}, bf16[64,4096]{1,0:T(8,128)(2,1)S(1)}, u32[]{:S(2)}, u32[]{:S(2)}) %collective-permute-start.7) | collective-permute-done | bytes 524320 | tf_op jit(solution)/shard_map/ppermute | solution.py:40
  191.8 23.9 %project_attend.1 = bf16[1024,512]{1,0:T(8,128)(2,1)} custom-call(s32[13]{0:T(128)S(1)} %stack.55.row_ref, s32[64]{0:T(128)S(1)} %fusion.4.pos_ref, s32[1]{0:T(128)S(6)} %copy.28.len_ref, bf16[128,4096]{1,0:T(8,128)(2,1)S(1)} %bitcast.27, bf16[128,4096]{1,0:T(8,128)(2,1)S(1)} %collective-permute-done.refs_1_, ...), custom_call_target="tpu_custom_call" | custom-call | tf_op jit(solution)/shard_map/project_attend/pallas_call | solution.py:197
  (48 shorter events, 20.2 us)
Async XLA Ops:
  2.5 11.2 %collective-permute-start.12 = (bf16[1,64,768]{2,1,0:T(8,128)(2,1)S(1)}, bf16[1,64,768]{2,1,0:T(8,128)(2,1)S(1)}, u32[]{:S(2)}, u32[]{:S(2)}) collective-permute-start(bf16[1,64,768]{2,1,0:T(8,128)(2,1)S(1)} %get-tuple-element.7), channel_id=1, source_target_pairs={{0,128},{8,136},{16,144},{24,152},{32,160},{40,168},{48,176},{56,1... | collective-permute-start | bytes 294920 | tf_op jit(solution)/shard_map/ppermute | solution.py:36
  6.5 7.2 %collective-permute-start.13 = (bf16[1,64,768]{2,1,0:T(8,128)(2,1)S(1)}, bf16[1,64,768]{2,1,0:T(8,128)(2,1)S(1)}, u32[]{:S(2)}, u32[]{:S(2)}) collective-permute-start(bf16[1,64,768]{2,1,0:T(8,128)(2,1)S(1)} %get-tuple-element.7), channel_id=1, source_target_pairs={{0,256},{8,264},{16,272},{24,280},{32,288},{40,296},{48,304},{56,3... | collective-permute-start | bytes 294920 | tf_op jit(solution)/shard_map/ppermute | solution.py:36
  10.7 7.6 %collective-permute-start.14 = (bf16[1,64,768]{2,1,0:T(8,128)(2,1)S(1)}, bf16[1,64,768]{2,1,0:T(8,128)(2,1)S(1)}, u32[]{:S(2)}, u32[]{:S(2)}) collective-permute-start(bf16[1,64,768]{2,1,0:T(8,128)(2,1)S(1)} %get-tuple-element.7), channel_id=1, source_target_pairs={{0,384},{8,392},{16,400},{24,408},{32,416},{40,424},{48,432},{56,4... | collective-permute-start | bytes 294920 | tf_op jit(solution)/shard_map/ppermute | solution.py:36
  19.2 61.2 %copy-start = (bf16[1,128,4096]{2,1,0:T(8,128)(2,1)S(1)}, bf16[1,128,4096]{2,1,0:T(8,128)(2,1)}, u32[]{:S(2)}) copy-start(bf16[1,128,4096]{2,1,0:T(8,128)(2,1)} %param.9) | copy-start | bytes 3145732
  19.2 17.6 %collective-permute-start.15 = (bf16[4,64,768]{2,1,0:T(8,128)(2,1)S(1)}, bf16[4,64,768]{2,1,0:T(8,128)(2,1)S(1)}, u32[]{:S(2)}, u32[]{:S(2)}) collective-permute-start(bf16[4,64,768]{2,1,0:T(8,128)(2,1)S(1)} %pad_maximum_fusion.2), channel_id=1, source_target_pairs={{0,16},{8,24},{16,32},{24,40},{32,48},{40,56},{48,64},{56,72},{64,... | collective-permute-start | bytes 1179656 | tf_op jit(solution)/shard_map/ppermute | solution.py:36
  36.8 11.8 %collective-permute-start.16 = (bf16[4,64,768]{2,1,0:T(8,128)(2,1)S(1)}, bf16[4,64,768]{2,1,0:T(8,128)(2,1)S(1)}, u32[]{:S(2)}, u32[]{:S(2)}) collective-permute-start(bf16[4,64,768]{2,1,0:T(8,128)(2,1)S(1)} %collective-permute-done.15), channel_id=1, source_target_pairs={{0,16},{8,24},{16,32},{24,40},{32,48},{40,56},{48,64},{56,72},{64,... | collective-permute-start | bytes 1179656 | tf_op jit(solution)/shard_map/ppermute | solution.py:36
  38.7 11.8 %collective-permute-start.19 = (bf16[4,64,768]{2,1,0:T(8,128)(2,1)S(1)}, bf16[4,64,768]{2,1,0:T(8,128)(2,1)S(1)}, u32[]{:S(2)}, u32[]{:S(2)}) collective-permute-start(bf16[4,64,768]{2,1,0:T(8,128)(2,1)S(1)} %pad_maximum_fusion.2), channel_id=1, source_target_pairs={{0,112},{8,120},{16,0},{24,8},{32,16},{40,24},{48,32},{56,40},{64,... | collective-permute-start | bytes 1179656 | tf_op jit(solution)/shard_map/ppermute | solution.py:36
  48.6 10.9 %collective-permute-start.17 = (bf16[4,64,768]{2,1,0:T(8,128)(2,1)S(1)}, bf16[4,64,768]{2,1,0:T(8,128)(2,1)S(1)}, u32[]{:S(2)}, u32[]{:S(2)}) collective-permute-start(bf16[4,64,768]{2,1,0:T(8,128)(2,1)S(1)} %collective-permute-done.16), channel_id=1, source_target_pairs={{0,16},{8,24},{16,32},{24,40},{32,48},{40,56},{48,64},{56,72},{64,... | collective-permute-start | bytes 1179656 | tf_op jit(solution)/shard_map/ppermute | solution.py:36
  50.5 11.5 %collective-permute-start.20 = (bf16[4,64,768]{2,1,0:T(8,128)(2,1)S(1)}, bf16[4,64,768]{2,1,0:T(8,128)(2,1)S(1)}, u32[]{:S(2)}, u32[]{:S(2)}) collective-permute-start(bf16[4,64,768]{2,1,0:T(8,128)(2,1)S(1)} %collective-permute-done.19), channel_id=1, source_target_pairs={{0,112},{8,120},{16,0},{24,8},{32,16},{40,24},{48,32},{56,40},{64,... | collective-permute-start | bytes 1179656 | tf_op jit(solution)/shard_map/ppermute | solution.py:36
  59.5 10.1 %collective-permute-start.18 = (bf16[4,64,768]{2,1,0:T(8,128)(2,1)S(1)}, bf16[4,64,768]{2,1,0:T(8,128)(2,1)S(1)}, u32[]{:S(2)}, u32[]{:S(2)}) collective-permute-start(bf16[4,64,768]{2,1,0:T(8,128)(2,1)S(1)} %collective-permute-done.17), channel_id=1, source_target_pairs={{0,16},{8,24},{16,32},{24,40},{32,48},{40,56},{48,64},{56,72},{64,... | collective-permute-start | bytes 1179656 | tf_op jit(solution)/shard_map/ppermute | solution.py:36
  62.1 9.3 %collective-permute-start.21 = (bf16[4,64,768]{2,1,0:T(8,128)(2,1)S(1)}, bf16[4,64,768]{2,1,0:T(8,128)(2,1)S(1)}, u32[]{:S(2)}, u32[]{:S(2)}) collective-permute-start(bf16[4,64,768]{2,1,0:T(8,128)(2,1)S(1)} %collective-permute-done.20), channel_id=1, source_target_pairs={{0,112},{8,120},{16,0},{24,8},{32,16},{40,24},{48,32},{56,40},{64,... | collective-permute-start | bytes 1179656 | tf_op jit(solution)/shard_map/ppermute | solution.py:36
  68.2 84.4 %copy-start.1 = (f32[512]{0:T(512)S(1)}, f32[512]{0:T(512)}, u32[]{:S(2)}) copy-start(f32[512]{0:T(512)} %param.13) | copy-start | bytes 6148
  73.7 118.1 %collective-permute-start.22 = (bf16[32,64,768]{2,1,0:T(8,128)(2,1)}, bf16[32,64,768]{2,1,0:T(8,128)(2,1)}, u32[]{:S(2)}, u32[]{:S(2)}) collective-permute-start(bf16[32,64,768]{2,1,0:T(8,128)(2,1)} %constant_dynamic-update-slice_fusion.refs_13_), channel_id=1, source_target_pairs={{0,8},{8,0},{16,24},{24,16},{32,40},{40,32},{48,56},{56,48},{64,72... | collective-permute-start | bytes 9437192 | tf_op jit(solution)/shard_map/ppermute | solution.py:36
  80.4 63.9 %collective-permute-start = (bf16[128,4096]{1,0:T(8,128)(2,1)S(1)}, bf16[128,4096]{1,0:T(8,128)(2,1)S(1)}, u32[]{:S(2)}, u32[]{:S(2)}) collective-permute-start(bf16[128,4096]{1,0:T(8,128)(2,1)S(1)} %bitcast.25), channel_id=1, source_target_pairs={{0,1},{1,2},{2,3},{3,0},{4,5},{5,6},{6,7},{7,4},{8,9},{9,10},{10,1... | collective-permute-start | bytes 3145736 | tf_op jit(solution)/shard_map/ppermute | solution.py:40
  83.6 65.4 %collective-permute-start.1 = (bf16[128,4096]{1,0:T(8,128)(2,1)S(1)}, bf16[128,4096]{1,0:T(8,128)(2,1)S(1)}, u32[]{:S(2)}, u32[]{:S(2)}) collective-permute-start(bf16[128,4096]{1,0:T(8,128)(2,1)S(1)} %bitcast.26), channel_id=1, source_target_pairs={{0,3},{1,0},{2,1},{3,2},{4,7},{5,4},{6,5},{7,6},{8,11},{9,8},{10,9... | collective-permute-start | bytes 3145736 | tf_op jit(solution)/shard_map/ppermute | solution.py:40
  87.0 38.5 %collective-permute-start.8 = (bf16[64,4096]{1,0:T(8,128)(2,1)S(1)}, bf16[64,4096]{1,0:T(8,128)(2,1)}, u32[]{:S(2)}, u32[]{:S(2)}) collective-permute-start(bf16[64,4096]{1,0:T(8,128)(2,1)S(1)} %get-tuple-element.5), channel_id=1, source_target_pairs={{0,4},{1,5},{2,6},{3,7},{4,0},{5,1},{6,2},{7,3},{8,12},{9,13},{10,... | collective-permute-start | bytes 1572872 | tf_op jit(solution)/shard_map/ppermute | solution.py:40
  96.7 45.7 %collective-permute-start.4 = (bf16[64,4096]{1,0:T(8,128)(2,1)S(1)}, bf16[64,4096]{1,0:T(8,128)(2,1)}, u32[]{:S(2)}, u32[]{:S(2)}) collective-permute-start(bf16[64,4096]{1,0:T(8,128)(2,1)S(1)} %get-tuple-element.6), channel_id=1, source_target_pairs={{0,4},{1,5},{2,6},{3,7},{4,0},{5,1},{6,2},{7,3},{8,12},{9,13},{10,... | collective-permute-start | bytes 1572872 | tf_op jit(solution)/shard_map/ppermute | solution.py:40
  125.6 27.9 %collective-permute-start.10 = (bf16[64,4096]{1,0:T(8,128)(2,1)}, bf16[64,4096]{1,0:T(8,128)(2,1)}, u32[]{:S(2)}, u32[]{:S(2)}) collective-permute-start(bf16[64,4096]{1,0:T(8,128)(2,1)} %collective-permute-done.8.refs_9_), channel_id=1, source_target_pairs={{0,3},{1,0},{2,1},{3,2},{4,7},{5,4},{6,5},{7,6},{8,11},{9,8},{10,9... | collective-permute-start | bytes 1572872 | tf_op jit(solution)/shard_map/ppermute | solution.py:40
  142.4 15.7 %collective-permute-start.5 = (bf16[64,4096]{1,0:T(8,128)(2,1)}, bf16[64,4096]{1,0:T(8,128)(2,1)}, u32[]{:S(2)}, u32[]{:S(2)}) collective-permute-start(bf16[64,4096]{1,0:T(8,128)(2,1)} %collective-permute-done.4.refs_5_), channel_id=1, source_target_pairs={{0,1},{1,2},{2,3},{3,0},{4,5},{5,6},{6,7},{7,4},{8,9},{9,10},{10,1... | collective-permute-start | bytes 1572872 | tf_op jit(solution)/shard_map/ppermute | solution.py:40
  144.4 15.7 %collective-permute-start.6 = (bf16[64,4096]{1,0:T(8,128)(2,1)}, bf16[64,4096]{1,0:T(8,128)(2,1)}, u32[]{:S(2)}, u32[]{:S(2)}) collective-permute-start(bf16[64,4096]{1,0:T(8,128)(2,1)} %collective-permute-done.4.refs_5_), channel_id=1, source_target_pairs={{0,3},{1,0},{2,1},{3,2},{4,7},{5,4},{6,5},{7,6},{8,11},{9,8},{10,9... | collective-permute-start | bytes 1572872 | tf_op jit(solution)/shard_map/ppermute | solution.py:40
  149.0 20.4 %collective-permute-start.9 = (bf16[64,4096]{1,0:T(8,128)(2,1)}, bf16[64,4096]{1,0:T(8,128)(2,1)}, u32[]{:S(2)}, u32[]{:S(2)}) collective-permute-start(bf16[64,4096]{1,0:T(8,128)(2,1)} %collective-permute-done.8.refs_9_), channel_id=1, source_target_pairs={{0,1},{1,2},{2,3},{3,0},{4,5},{5,6},{6,7},{7,4},{8,9},{9,10},{10,1... | collective-permute-start | bytes 1572872 | tf_op jit(solution)/shard_map/ppermute | solution.py:40
  153.4 20.2 %copy-start.2 = (s32[64]{0:T(128)S(1)}, s32[64]{0:T(128)}, u32[]{:S(2)}) copy-start(s32[64]{0:T(128)} %param.16) | copy-start | bytes 772
  153.5 38.2 %collective-permute-start.2 = (bf16[64,4096]{1,0:T(8,128)(2,1)S(1)}, bf16[64,4096]{1,0:T(8,128)(2,1)S(1)}, u32[]{:S(2)}, u32[]{:S(2)}) collective-permute-start(bf16[64,4096]{1,0:T(8,128)(2,1)S(1)} %slice.24), channel_id=1, source_target_pairs={{0,1},{1,2},{2,3},{3,0},{4,5},{5,6},{6,7},{7,4},{8,9},{9,10},{10,1... | collective-permute-start | bytes 1572872 | tf_op jit(solution)/shard_map/ppermute | solution.py:40
  158.1 33.6 %collective-permute-start.3 = (bf16[64,4096]{1,0:T(8,128)(2,1)S(1)}, bf16[64,4096]{1,0:T(8,128)(2,1)S(1)}, u32[]{:S(2)}, u32[]{:S(2)}) collective-permute-start(bf16[64,4096]{1,0:T(8,128)(2,1)S(1)} %slice.25), channel_id=1, source_target_pairs={{0,3},{1,0},{2,1},{3,2},{4,7},{5,4},{6,5},{7,6},{8,11},{9,8},{10,9... | collective-permute-start | bytes 1572872 | tf_op jit(solution)/shard_map/ppermute | solution.py:40
  160.1 20.9 %collective-permute-start.11 = (bf16[64,4096]{1,0:T(8,128)(2,1)}, bf16[64,4096]{1,0:T(8,128)(2,1)S(1)}, u32[]{:S(2)}, u32[]{:S(2)}) collective-permute-start(bf16[64,4096]{1,0:T(8,128)(2,1)} %collective-permute-done.10.refs_11_), channel_id=1, source_target_pairs={{0,3},{1,0},{2,1},{3,2},{4,7},{5,4},{6,5},{7,6},{8,11},{9,8},{10,9... | collective-permute-start | bytes 1572872 | tf_op jit(solution)/shard_map/ppermute | solution.py:40
  169.4 22.4 %collective-permute-start.7 = (bf16[64,4096]{1,0:T(8,128)(2,1)}, bf16[64,4096]{1,0:T(8,128)(2,1)S(1)}, u32[]{:S(2)}, u32[]{:S(2)}) collective-permute-start(bf16[64,4096]{1,0:T(8,128)(2,1)} %collective-permute-done.5.refs_6_), channel_id=1, source_target_pairs={{0,1},{1,2},{2,3},{3,0},{4,5},{5,6},{6,7},{7,4},{8,9},{9,10},{10,1... | collective-permute-start | bytes 1572872 | tf_op jit(solution)/shard_map/ppermute | solution.py:40
